TPU v7x, 512 devices: a whole 4x8x8 slice. The times are simulated.
512 devices in a mesh: sen: 32 (over y, z_hi), par: 16 (over x, z_lo, core).
Axes of the slice: x: 4, y: 8, z: 8 (z_hi: 4, z_lo: 2; z = z_hi * 2 + z_lo), core: 2. Of those that a mesh axis runs over, the one named last changes fastest.
Arguments:
- vectors: float32 [2, 256, 256], P(None, 'sen'), may hold values from -6 to 6
- observed: float32 [2, 256, 256], P(None, 'sen'), may hold values from -6 to 6
- operator: bfloat16 [2, 128, 256, 6144], P(None, None, 'sen', 'par'), may hold values from -0.15625 to 0.15625
- noise: float32 [256], P('sen'), may hold values from 0.3 to 3
- coefficient: float32 [16, 384], P('par'), may hold values from 0.05 to 0.24
- offsets: int32 [16, 384], P('par'), may hold values from -3 to 3
Outputs:
- residual: float32 [2, 256, 256], P(None, 'sen')
- applied: float32 [2, 256, 256], P(None, 'sen')
All inputs are finite; a program needn't handle non-finite values.
Results may differ from a plain program's by a relative error of at most 0.0018.
Values may be sent and summed in bfloat16 or wider, within the bound.
A program may use at most 64 MiB of HBM per device.

v0:
```python
import math
import jax
import jax.numpy as jnp
from jax import lax
from jax.sharding import PartitionSpec as P

SWEEPS = 4


def make_basis(length):
    half = length // 2
    times = jnp.arange(length, dtype=jnp.int32)[:, None]
    freqs = jnp.arange(half, dtype=jnp.int32)[None, :]
    phase = (2 * freqs + 1) * times % (2 * length)
    angle = phase.astype(jnp.float32) * (math.pi / length)
    scale = math.sqrt(2.0 / length)
    return jnp.concatenate([jnp.cos(angle), jnp.sin(angle)], axis=1) * scale


def smooth(field, coefficient, offsets):
    width = field.shape[-1]
    for sweep in range(SWEEPS):
        padded = jnp.pad(field, ((1, 1), (0, 0)))
        upper = padded[:-2]
        lower_pad = jnp.pad(padded[2:], ((0, 0), (3, 3)))
        linked = jnp.zeros_like(field)
        for shift in range(-3, 4):
            linked = linked + jnp.where(
                offsets == shift, lower_pad[:, 3 + shift : 3 + shift + width], 0.0
            )
        sides = jnp.pad(field, ((0, 0), (1, 1)))
        field = field + coefficient * (sides[:, :-2] + sides[:, 2:] + upper + linked - 4.0 * field)
    return field


def hessian(record, operator, noise, coefficient, offsets, basis):
    rows, sensors, length = record.shape
    half = length // 2
    cells = operator.shape[-1]
    spectrum = jnp.dot(
        record.reshape(rows * sensors, length), basis, precision=lax.Precision.HIGHEST
    )
    spectrum = spectrum.reshape(rows, sensors, 2, half).transpose(2, 3, 0, 1).astype(jnp.bfloat16)
    real = jnp.einsum(
        "frs,fsp->frp", spectrum[0], operator[0], preferred_element_type=jnp.float32
    ) + jnp.einsum("frs,fsp->frp", spectrum[1], operator[1], preferred_element_type=jnp.float32)
    imag = jnp.einsum(
        "frs,fsp->frp", spectrum[1], operator[0], preferred_element_type=jnp.float32
    ) - jnp.einsum("frs,fsp->frp", spectrum[0], operator[1], preferred_element_type=jnp.float32)
    planes = jnp.stack([real, imag], axis=1).reshape(half * 2 * rows, cells)
    planes = lax.psum_scatter(planes, "sen", scatter_dimension=0, tiled=True)
    plane = lax.all_to_all(planes, "par", 0, 0, tiled=True)
    prior = smooth(plane, coefficient, offsets).astype(jnp.bfloat16)
    planes = lax.all_to_all(prior, "par", 0, 0, tiled=True)
    planes = lax.all_gather(planes, "sen", axis=0, tiled=True)
    planes = planes.reshape(half, 2, rows, cells)
    flat = (planes[:, 0], planes[:, 1])
    real = jnp.einsum(
        "fsp,frp->frs", operator[0], flat[0], preferred_element_type=jnp.float32
    ) - jnp.einsum("fsp,frp->frs", operator[1], flat[1], preferred_element_type=jnp.float32)
    imag = jnp.einsum(
        "fsp,frp->frs", operator[0], flat[1], preferred_element_type=jnp.float32
    ) + jnp.einsum("fsp,frp->frs", operator[1], flat[0], preferred_element_type=jnp.float32)
    forward = lax.psum(jnp.stack([real, imag]), "par")
    forward = forward.transpose(2, 3, 0, 1).reshape(rows * sensors, length)
    back = jnp.dot(forward, basis.T, precision=lax.Precision.HIGHEST).reshape(rows, sensors, length)
    return back + noise[None, :, None] * record


def body(vectors, observed, operator, noise, coefficient, offsets):
    basis = make_basis(vectors.shape[-1])
    coefficient = lax.all_gather(coefficient, "par", axis=0, tiled=True)
    offsets = lax.all_gather(offsets, "par", axis=0, tiled=True)
    residual = observed - hessian(vectors, operator, noise, coefficient, offsets, basis)
    applied = hessian(residual, operator, noise, coefficient, offsets, basis)
    return (residual, applied)


def solution(mesh):
    placed = (
        P(None, "sen", None),
        P(None, "sen", None),
        P(None, None, "sen", "par"),
        P("sen"),
        P("par", None),
        P("par", None),
    )
    return jax.shard_map(
        body,
        mesh=mesh,
        in_specs=placed,
        out_specs=(P(None, "sen", None), P(None, "sen", None)),
        check_vma=False,
    )
```

profile of v0, /device:TPU:32, one launch (start us, length us, event | category | flops | bytes accessed | tf_op | source)
XLA Modules:
  0.0 826.7 jit_solution(6979798992075680855)
XLA Ops:
  7.2 0.5 fusion.60
  7.8 0.9 fusion.9
  8.7 0.2 copy.59
  8.9 1.5 fusion.32
  10.5 0.4 fusion.30
  10.9 0.4 fusion.3
  11.3 0.4 fusion.2
  11.8 0.3 pad_maximum_fusion
  12.1 0.3 copy.60
  12.4 1.4 reshape.51
  13.9 231.9 %reduce-scatter.3.cloned.1.call-done = f32[16,384]{1,0:T(8,128)} async-done(((f32[512,384]{1,0:T(8,128)}), f32[16,384]{1,0:T(8,128)}) %reduce-scatter.3.cloned.1.call-update) | async-done | bytes 24592 | tf_op jit(solution)/shard_map/reduce_scatter | solution.py:51
  245.8 1.4 copy.61
  247.1 4.6 all-to-all-start
  251.7 20.0 %all-gather.2 = f32[16,1,384]{2,1,0:T(1,128)S(1)} all-gather(f32[1,1,384]{2,1,0:T(1,128)S(1)} %bitcast.259), channel_id=1, replica_groups=mesh['sen'=32,'par'=16] {'par'}, dimensions={0}, use_global_device_ids=true | all-gather | bytes 26112 | tf_op jit(solution)/shard_map/all_gather | solution.py:72
  271.8 16.3 %all-gather.3 = s32[16,1,384]{2,1,0:T(1,128)S(1)} all-gather(s32[1,1,384]{2,1,0:T(1,128)S(1)} %bitcast.260), channel_id=1, replica_groups=mesh['sen'=32,'par'=16] {'par'}, dimensions={0}, use_global_device_ids=true | all-gather | bytes 26112 | tf_op jit(solution)/shard_map/all_gather | solution.py:73
  288.1 0.1 fusion.66
  288.3 0.1 fusion.72
  288.4 0.1 fusion.78
  288.6 0.1 fusion.210
  288.7 0.6 broadcast.143
  289.3 0.6 reduce
  289.9 0.7 reshape.80
  290.6 3.5 all-to-all-start.1
  294.2 0.1 copy.91
  294.3 5.8 all-to-all-done.1
  300.1 0.1 reshape.81
  300.2 80.9 %all-gather = bf16[512,1,384]{2,0,1:T(8,128)(2,1)S(1)} all-gather(bf16[16,1,384]{2,0,1:T(8,128)(2,1)S(1)} %copy.70), channel_id=2, replica_groups=mesh['sen'=32,'par'=16] {'sen'}, dimensions={0}, use_global_device_ids=true | all-gather | bytes 405504 | tf_op jit(solution)/shard_map/all_gather | solution.py:55
  381.1 0.1 reshape.52
  381.3 0.5 fusion.28
  381.8 0.6 fusion.26
  382.4 0.6 fusion.7
  383.0 0.4 fusion.6
  383.5 52.9 %psum.14 = f32[2,8,256]{2,1,0:T(8,128)S(1)} all-reduce(f32[2,8,256]{2,1,0:T(8,128)S(1)} %copy_bitcast_fusion.3), channel_id=1, replica_groups=mesh['sen'=32,'par'=16] {'par'}, use_global_device_ids=true, to_apply=%region_1.2 | all-reduce | flops 4096 | bytes 32768 | tf_op jit(solution)/shard_map/psum | solution.py:64
  436.4 0.3 fusion.8
  436.7 0.3 convolution_convert_fusion
  437.1 0.1 copy.77
  437.2 0.4 fusion.24
  437.6 0.1 copy.78
  437.8 0.4 fusion.22
  438.2 0.4 fusion.1
  438.6 0.4 fusion
  439.0 0.3 pad_maximum_fusion.1
  439.4 0.3 copy.81
  439.7 1.4 reshape.53
  441.1 220.9 %reduce-scatter.5.cloned.1.call-done = f32[16,384]{1,0:T(8,128)} async-done(((f32[512,384]{1,0:T(8,128)}), f32[16,384]{1,0:T(8,128)}) %reduce-scatter.5.cloned.1.call-update) | async-done | bytes 24592 | tf_op jit(solution)/shard_map/reduce_scatter | solution.py:51
  662.1 0.8 copy.82
  662.8 10.4 %all_to_all.48 = f32[16,1,384]{2,1,0:T(1,128)S(1)} all-to-all(f32[16,1,384]{2,1,0:T(1,128)S(1)} %copy.82), channel_id=1, replica_groups=mesh['sen'=32,'par'=16] {'par'}, dimensions={0} | all-to-all | bytes 49152 | tf_op jit(solution)/shard_map/all_to_all | solution.py:52
  673.3 0.1 fusion.91
  673.4 0.1 fusion.97
  673.5 0.1 fusion.103
  673.7 0.1 fusion.209
  673.8 0.6 reduce.1
  674.5 0.1 reshape.82
  674.5 8.6 %all_to_all.49 = bf16[16,2,192]{2,1,0:T(2,128)(2,1)S(1)} all-to-all(bf16[16,2,192]{2,1,0:T(2,128)(2,1)S(1)} %reshape.82), channel_id=1, replica_groups=mesh['sen'=32,'par'=16] {'par'}, dimensions={0} | all-to-all | bytes 24576 | tf_op jit(solution)/shard_map/all_to_all | solution.py:54
  683.2 0.1 reshape.83
  683.3 80.4 %all-gather.1 = bf16[512,1,384]{2,0,1:T(8,128)(2,1)S(1)} all-gather(bf16[16,1,384]{2,0,1:T(8,128)(2,1)S(1)} %copy.84), channel_id=3, replica_groups=mesh['sen'=32,'par'=16] {'sen'}, dimensions={0}, use_global_device_ids=true | all-gather | bytes 405504 | tf_op jit(solution)/shard_map/all_gather | solution.py:55
  763.6 0.1 reshape.54
  763.8 0.5 fusion.20
  764.3 0.6 fusion.18
  764.9 0.6 fusion.5
  765.5 0.1 copy.87
  765.5 0.4 fusion.4
  766.0 52.9 %psum.15 = f32[2,8,256]{2,1,0:T(8,128)S(1)} all-reduce(f32[2,8,256]{2,1,0:T(8,128)S(1)} %copy_bitcast_fusion.2), channel_id=1, replica_groups=mesh['sen'=32,'par'=16] {'par'}, use_global_device_ids=true, to_apply=%region_3.4 | all-reduce | flops 4096 | bytes 32768 | tf_op jit(solution)/shard_map/psum | solution.py:64
  818.9 0.9 convolution_add_fusion.4
  (39 shorter events, 0.5 us)
Async XLA Ops:
  7.2 3.3 copy-start
  7.2 238.6 %reduce-scatter.3.cloned.1.call-start = ((), (), s32[]{:S(2)}) async-start(), calls=%async_computation.6 | async-start | bytes 811008 | tf_op jit(solution)/shard_map/reduce_scatter | solution.py:51
  12.4 239.4 %copy-start.5 = (f32[1,384]{1,0:T(1,128)S(1)}, f32[1,384]{1,0:T(1,128)}, u32[]{:S(2)}) copy-start(f32[1,384]{1,0:T(1,128)} %param.10) | copy-start | bytes 4612
  12.4 259.4 %copy-start.6 = (s32[1,384]{1,0:T(1,128)S(1)}, s32[1,384]{1,0:T(1,128)}, u32[]{:S(2)}) copy-start(s32[1,384]{1,0:T(1,128)} %param.11) | copy-start | bytes 4612
  247.1 41.0 %all-to-all-start = ((f32[16,1,384]{2,1,0:T(1,128)}), f32[16,1,384]{2,1,0:T(1,128)S(1)}, u32[]{:S(2)}, u32[]{:S(2)}) async-start(f32[16,1,384]{2,1,0:T(1,128)} %copy.61), calls=%async_computation.1 | async-start | bytes 49152 | tf_op jit(solution)/shard_map/all_to_all | solution.py:52
  290.6 9.5 %all-to-all-start.1 = ((bf16[16,2,192]{2,1,0:T(2,128)(2,1)}), bf16[16,2,192]{2,1,0:T(2,128)(2,1)S(1)}, u32[]{:S(2)}, u32[]{:S(2)}) async-start(bf16[16,2,192]{2,1,0:T(2,128)(2,1)} %reshape.80), calls=%async_computation.2 | async-start | bytes 32768 | tf_op jit(solution)/shard_map/all_to_all | solution.py:54
  294.1 368.0 %reduce-scatter.5.cloned.1.call-start = ((), (), s32[]{:S(2)}) async-start(), calls=%async_computation.7 | async-start | bytes 811008 | tf_op jit(solution)/shard_map/reduce_scatter | solution.py:51
  382.9 53.5 %copy-start.2 = (f32[2,8,256]{2,1,0:T(8,128)S(1)}, f32[2,8,256]{2,1,0:T(8,128)}, u32[]{:S(2)}) copy-start(f32[2,8,256]{2,1,0:T(8,128)} %param.6) | copy-start | bytes 49156
  382.9 53.5 %copy-start.3 = (f32[2,8,256]{2,1,0:T(8,128)S(1)}, f32[2,8,256]{2,1,0:T(8,128)}, u32[]{:S(2)}) copy-start(f32[2,8,256]{2,1,0:T(8,128)} %param.7) | copy-start | bytes 49156
  382.9 53.5 %copy-start.4 = (f32[8]{0:T(128)S(1)}, f32[8]{0:T(128)}, u32[]{:S(2)}) copy-start(f32[8]{0:T(128)} %param.9) | copy-start | bytes 100
  436.7 382.2 %copy-start.1 = (f32[2,8,256]{2,1,0:T(8,128)}, f32[2,8,256]{2,1,0:T(8,128)S(1)}, u32[]{:S(2)}) copy-start(f32[2,8,256]{2,1,0:T(8,128)S(1)} %fusion.8) | copy-start | bytes 49156
Sparse Core Ops, SparseCore 0:
  14.0 231.7 reduce-scatter.2
  441.2 220.7 reduce-scatter.4
where the time goes:
time: 827 us
  waiting for transfers between devices  459 us (56%)
  blocking collectives  322 us (39%)
  between operations  14.4 us (2%)
  matrix products  11.1 us (1%)
  local copies, waits for them, and re-layouts  8.35 us (1%)
    reduce_scatter x2, waiting for transfers between devices, hessian(): planes = lax.psum_scatter(planes, 'sen', scatter_dimension=0, tiled=True)  453 us
    all_gather x2, blocking collectives, hessian(): planes = lax.all_gather(planes, 'sen', axis=0, tiled=True)  161 us
    psum x2, blocking collectives, hessian(): forward = lax.psum(jnp.stack([real, imag]), 'par')  106 us
    all_gather x1, blocking collectives, body(): coefficient = lax.all_gather(coefficient, 'par', axis=0, tiled=True)  20 us
  transfers between devices with their start and end apart: 4, of which 3 were waited for; matrix products, arithmetic and copies ran while one was open for 0% of the time, Pallas kernels for 0%

commit v1 on v0

--- a/solution.py
+++ b/solution.py
@@ -61,7 +61,7 @@
     imag = jnp.einsum(
         "fsp,frp->frs", operator[0], flat[1], preferred_element_type=jnp.float32
     ) + jnp.einsum("fsp,frp->frs", operator[1], flat[0], preferred_element_type=jnp.float32)
-    forward = lax.psum(jnp.stack([real, imag]), "par")
+    forward = jnp.sum(lax.all_gather(jnp.stack([real, imag]), "par"), axis=0)
     forward = forward.transpose(2, 3, 0, 1).reshape(rows * sensors, length)
     back = jnp.dot(forward, basis.T, precision=lax.Precision.HIGHEST).reshape(rows, sensors, length)
     return back + noise[None, :, None] * record

time: 827 us -> 763 us (0.923)
  the two profiles are of different devices: /device:TPU:32 before, /device:TPU:1 now
where the time goes in v1:
time: 763 us; the launch traced here: 762 us
  waiting for transfers between devices  451 us (59%)
  blocking collectives  260 us (34%)
  between operations  14.4 us (2%)
  starting transfers between devices  13.4 us (2%)
  matrix products  11.6 us (2%)
  local copies, waits for them, and re-layouts  8.64 us (1%)
    reduce_scatter x2, waiting for transfers between devices, hessian(): planes = lax.psum_scatter(planes, 'sen', scatter_dimension=0, tiled=True)  445 us
    all_gather x2, blocking collectives, hessian(): planes = lax.all_gather(planes, 'sen', axis=0, tiled=True)  134 us
    all_gather x2, blocking collectives, hessian(): forward = jnp.sum(lax.all_gather(jnp.stack([real, imag]), 'par'), axis=0)  65.2 us
    all_gather x1, blocking collectives, body(): coefficient = lax.all_gather(coefficient, 'par', axis=0, tiled=True)  20 us
    all_gather x1, blocking collectives, body(): offsets = lax.all_gather(offsets, 'par', axis=0, tiled=True)  16.3 us
    all_to_all x1, blocking collectives, hessian(): plane = lax.all_to_all(planes, 'par', 0, 0, tiled=True)  15.4 us
  transfers between devices with their start and end apart: 4, of which 3 were waited for; matrix products, arithmetic and copies ran while one was open for 0% of the time, Pallas kernels for 0%

profile of v1, /device:TPU:1, one launch (start us, length us, event | category | flops | bytes accessed | tf_op | source)
XLA Modules:
  0.0 762.0 jit_solution(10286224302894703567)
XLA Ops:
  7.2 0.5 fusion.62
  7.8 0.9 fusion.9
  8.7 0.2 copy.57
  8.9 1.6 fusion.32
  10.5 0.4 fusion.30
  10.9 0.4 fusion.3
  11.3 0.4 fusion.2
  11.8 0.3 pad_maximum_fusion
  12.1 0.3 copy.58
  12.4 1.4 reshape.51
  13.9 229.5 %reduce-scatter.3.cloned.1.call-done = f32[16,384]{1,0:T(8,128)} async-done(((f32[512,384]{1,0:T(8,128)}), f32[16,384]{1,0:T(8,128)}) %reduce-scatter.3.cloned.1.call-update) | async-done | bytes 24592 | tf_op jit(solution)/shard_map/reduce_scatter | solution.py:51
  243.4 1.4 copy.59
  244.7 9.8 %all-to-all-start = ((f32[16,1,384]{2,1,0:T(1,128)}), f32[16,1,384]{2,1,0:T(1,128)S(1)}, u32[]{:S(2)}, u32[]{:S(2)}) async-start(f32[16,1,384]{2,1,0:T(1,128)} %copy.59), calls=%async_computation.1 | async-start | bytes 49152 | tf_op jit(solution)/shard_map/all_to_all | solution.py:52
  254.6 20.0 %all-gather.4 = f32[16,1,384]{2,1,0:T(1,128)S(1)} all-gather(f32[1,1,384]{2,1,0:T(1,128)S(1)} %bitcast.259), channel_id=1, replica_groups=mesh['sen'=32,'par'=16] {'par'}, dimensions={0}, use_global_device_ids=true | all-gather | bytes 26112 | tf_op jit(solution)/shard_map/all_gather | solution.py:72
  274.6 16.3 %all-gather.5 = s32[16,1,384]{2,1,0:T(1,128)S(1)} all-gather(s32[1,1,384]{2,1,0:T(1,128)S(1)} %bitcast.260), channel_id=1, replica_groups=mesh['sen'=32,'par'=16] {'par'}, dimensions={0}, use_global_device_ids=true | all-gather | bytes 26112 | tf_op jit(solution)/shard_map/all_gather | solution.py:73
  290.9 0.1 fusion.68
  291.0 0.1 fusion.74
  291.2 0.1 fusion.80
  291.3 0.1 fusion.212
  291.5 0.6 broadcast.143
  292.0 0.6 reduce
  292.7 0.7 reshape.82
  293.4 3.4 all-to-all-start.1
  296.9 0.1 copy.91
  297.0 5.6 all-to-all-done.1
  302.7 0.1 reshape.83
  302.8 67.2 %all-gather = bf16[512,1,384]{2,0,1:T(8,128)(2,1)S(1)} all-gather(bf16[16,1,384]{2,0,1:T(8,128)(2,1)S(1)} %copy.68), channel_id=2, replica_groups=mesh['sen'=32,'par'=16] {'sen'}, dimensions={0}, use_global_device_ids=true | all-gather | bytes 405504 | tf_op jit(solution)/shard_map/all_gather | solution.py:55
  369.9 0.1 reshape.52
  370.1 0.5 fusion.28
  370.6 0.6 fusion.26
  371.2 0.6 fusion.7
  371.8 0.4 fusion.6
  372.3 32.6 %all-gather.1 = f32[32,128,2,8]{1,3,2,0:T(8,128)S(1)} all-gather(f32[2,128,2,8]{1,3,2,0:T(8,128)S(1)} %pad_maximum_fusion.2), channel_id=3, replica_groups=mesh['sen'=32,'par'=16] {'par'}, dimensions={0}, use_global_device_ids=true | all-gather | bytes 278528 | tf_op jit(solution)/shard_map/all_gather | solution.py:64
  405.0 0.1 copy.95
  405.1 0.5 fusion.8
  405.7 0.3 convolution_convert_fusion
  406.0 0.1 copy.76
  406.2 0.4 fusion.24
  406.6 0.1 copy.77
  406.7 0.4 fusion.22
  407.1 0.4 fusion.1
  407.6 0.4 fusion
  408.0 0.3 pad_maximum_fusion.1
  408.3 0.3 copy.80
  408.6 1.4 reshape.53
  410.1 215.4 %reduce-scatter.5.cloned.1.call-done = f32[16,384]{1,0:T(8,128)} async-done(((f32[512,384]{1,0:T(8,128)}), f32[16,384]{1,0:T(8,128)}) %reduce-scatter.5.cloned.1.call-update) | async-done | bytes 24592 | tf_op jit(solution)/shard_map/reduce_scatter | solution.py:51
  625.5 0.8 copy.81
  626.3 15.4 %all_to_all.48 = f32[16,1,384]{2,1,0:T(1,128)S(1)} all-to-all(f32[16,1,384]{2,1,0:T(1,128)S(1)} %copy.81), channel_id=1, replica_groups=mesh['sen'=32,'par'=16] {'par'}, dimensions={0} | all-to-all | bytes 49152 | tf_op jit(solution)/shard_map/all_to_all | solution.py:52
  641.6 0.1 fusion.93
  641.8 0.1 fusion.99
  641.9 0.1 fusion.105
  642.1 0.1 fusion.211
  642.2 0.6 reduce.1
  642.9 8.6 %all_to_all.49 = bf16[16,2,192]{2,1,0:T(2,128)(2,1)S(1)} all-to-all(bf16[16,2,192]{2,1,0:T(2,128)(2,1)S(1)} %reshape.84), channel_id=1, replica_groups=mesh['sen'=32,'par'=16] {'par'}, dimensions={0} | all-to-all | bytes 24576 | tf_op jit(solution)/shard_map/all_to_all | solution.py:54
  651.5 0.1 reshape.85
  651.7 67.2 %all-gather.2 = bf16[512,1,384]{2,0,1:T(8,128)(2,1)S(1)} all-gather(bf16[16,1,384]{2,0,1:T(8,128)(2,1)S(1)} %copy.83), channel_id=4, replica_groups=mesh['sen'=32,'par'=16] {'sen'}, dimensions={0}, use_global_device_ids=true | all-gather | bytes 405504 | tf_op jit(solution)/shard_map/all_gather | solution.py:55
  718.8 0.1 reshape.54
  719.0 0.5 fusion.20
  719.5 0.6 fusion.18
  720.1 0.6 fusion.5
  720.7 0.4 fusion.4
  721.2 32.6 %all-gather.3 = f32[32,128,2,8]{1,3,2,0:T(8,128)S(1)} all-gather(f32[2,128,2,8]{1,3,2,0:T(8,128)S(1)} %pad_maximum_fusion.3), channel_id=5, replica_groups=mesh['sen'=32,'par'=16] {'par'}, dimensions={0}, use_global_device_ids=true | all-gather | bytes 278528 | tf_op jit(solution)/shard_map/all_gather | solution.py:64
  753.8 0.1 copy.96
  754.0 1.2 convolution_add_fusion.4
  (43 shorter events, 0.7 us)
Async XLA Ops:
  7.2 3.3 copy-start
  7.2 236.2 %reduce-scatter.3.cloned.1.call-start = ((), (), s32[]{:S(2)}) async-start(), calls=%async_computation.6 | async-start | bytes 811008 | tf_op jit(solution)/shard_map/reduce_scatter | solution.py:51
  12.4 242.2 %copy-start.5 = (f32[1,384]{1,0:T(1,128)S(1)}, f32[1,384]{1,0:T(1,128)}, u32[]{:S(2)}) copy-start(f32[1,384]{1,0:T(1,128)} %param.10) | copy-start | bytes 4612
  12.4 262.2 %copy-start.6 = (s32[1,384]{1,0:T(1,128)S(1)}, s32[1,384]{1,0:T(1,128)}, u32[]{:S(2)}) copy-start(s32[1,384]{1,0:T(1,128)} %param.11) | copy-start | bytes 4612
  244.7 46.1 %all-to-all-start = ((f32[16,1,384]{2,1,0:T(1,128)}), f32[16,1,384]{2,1,0:T(1,128)S(1)}, u32[]{:S(2)}, u32[]{:S(2)}) async-start(f32[16,1,384]{2,1,0:T(1,128)} %copy.59), calls=%async_computation.1 | async-start | bytes 49152 | tf_op jit(solution)/shard_map/all_to_all | solution.py:52
  293.4 9.3 %all-to-all-start.1 = ((bf16[16,2,192]{2,1,0:T(2,128)(2,1)}), bf16[16,2,192]{2,1,0:T(2,128)(2,1)S(1)}, u32[]{:S(2)}, u32[]{:S(2)}) async-start(bf16[16,2,192]{2,1,0:T(2,128)(2,1)} %reshape.82), calls=%async_computation.2 | async-start | bytes 32768 | tf_op jit(solution)/shard_map/all_to_all | solution.py:54
  296.8 328.7 %reduce-scatter.5.cloned.1.call-start = ((), (), s32[]{:S(2)}) async-start(), calls=%async_computation.7 | async-start | bytes 811008 | tf_op jit(solution)/shard_map/reduce_scatter | solution.py:51
  371.8 33.3 %copy-start.2 = (f32[2,8,256]{2,1,0:T(8,128)S(1)}, f32[2,8,256]{2,1,0:T(8,128)}, u32[]{:S(2)}) copy-start(f32[2,8,256]{2,1,0:T(8,128)} %param.6) | copy-start | bytes 49156
  371.8 33.3 %copy-start.3 = (f32[2,8,256]{2,1,0:T(8,128)S(1)}, f32[2,8,256]{2,1,0:T(8,128)}, u32[]{:S(2)}) copy-start(f32[2,8,256]{2,1,0:T(8,128)} %param.7) | copy-start | bytes 49156
  371.8 33.3 %copy-start.4 = (f32[8]{0:T(128)S(1)}, f32[8]{0:T(128)}, u32[]{:S(2)}) copy-start(f32[8]{0:T(128)} %param.9) | copy-start | bytes 100
  405.7 348.3 %copy-start.1 = (f32[2,8,256]{2,1,0:T(8,128)}, f32[2,8,256]{2,1,0:T(8,128)S(1)}, u32[]{:S(2)}) copy-start(f32[2,8,256]{2,1,0:T(8,128)S(1)} %fusion.8) | copy-start | bytes 49156
Sparse Core Ops, SparseCore 0:
  14.0 229.3 reduce-scatter.2
  410.2 215.2 reduce-scatter.4
